TPU v7x, 32 devices: a whole 2x2x4 slice. The times are simulated.
32 devices in a mesh: grp: 2 (over x), ord: 16 (over z, y, core).
Axes of the slice: x: 2, y: 2, z: 4, core: 2. Of those that a mesh axis runs over, the one named last changes fastest.
Arguments:
- grid: bfloat16 [1024, 1024, 256], P(('grp', 'ord')), parts along dimension 0, may hold values from -6 to 6
- legendre: bfloat16 [16, 64, 512, 512], P('ord'), as said below
- mixing: bfloat16 [512, 2, 256, 256], P('ord'), may hold values from -0.25 to 0.25
Outputs:
- spectrum: bfloat16 [1024, 512, 512], P(('grp', 'ord')), parts along dimension 0
There are 2 independent parts, one for each index of `grp`. A program takes and returns all parts, laid end to end along the dimension named above; an argument that names none is the same for every part. Nothing has to cross between parts.
Inputs may be any that keep to these rules, and one draw needn't show every extreme that they name: `legendre`: entries whose degree is below their order are zero. The slots 32 to 63 of block index b repeat the panels that block index 16 - 1 - b holds in its slots 0 to 31.
All inputs are finite; a program needn't handle non-finite values.
Results may differ from a plain program's by a relative error of at most 0.0062.
Values may be sent and summed in bfloat16 or wider, within the bound.
No kernel may reach another device: no remote copies, remote signals or barrier semaphores. Data moves between devices by JAX's collectives and lax.ppermute only.
A program may use at most 256 MiB of HBM per device.

v0:
```python
import math
import jax
import jax.numpy as jnp
from jax import lax
from jax.sharding import PartitionSpec as P

DEG_TILE = 128


def fourier_table(nlon, orders):
    longitude = jnp.arange(nlon, dtype=jnp.int32)
    order = jnp.arange(orders, dtype=jnp.int32)
    phase = longitude[:, None] * order[None, :] % nlon
    angle = phase.astype(jnp.float32) * (2.0 * math.pi / nlon)
    scale = 1.0 / math.sqrt(nlon)
    table = jnp.stack([jnp.cos(angle) * scale, -jnp.sin(angle) * scale], axis=-1)
    return table.reshape(nlon, 2 * orders).astype(jnp.bfloat16)


def legendre_tiles(panel, arrived, first):
    groups, degrees, latitudes = panel.shape
    width = arrived.shape[2]
    buffer = jnp.zeros((groups, degrees, width), jnp.float32)

    def advance(index, current):
        start = index * DEG_TILE
        piece = lax.dynamic_slice_in_dim(panel, start, DEG_TILE, 1)
        part = jnp.einsum("mlt,tmk->mlk", piece, arrived, preferred_element_type=jnp.float32)
        return lax.dynamic_update_slice_in_dim(current, part, start, 1)

    return lax.fori_loop(first, degrees // DEG_TILE, advance, buffer).astype(jnp.bfloat16)


def on_device(grid, legendre, mixing):
    count = lax.axis_size("ord")
    block = lax.axis_index("ord")
    lat_rows, nlon, chans = grid.shape
    panels = legendre[0]
    per_dev = panels.shape[0] // 2
    orders = per_dev * count
    table = fourier_table(nlon, orders)
    spectra = jnp.einsum("tnc,nk->tkc", grid, table, preferred_element_type=jnp.float32).astype(
        jnp.bfloat16
    )
    sending = spectra.reshape(lat_rows, orders, 2 * chans)
    arrived = lax.all_to_all(sending, "ord", split_axis=1, concat_axis=0, tiled=True)
    first = per_dev * block // DEG_TILE
    coeffs = legendre_tiles(panels[:per_dev], arrived, first)
    landed = lax.all_to_all(coeffs, "ord", split_axis=1, concat_axis=0, tiled=True)
    real_part = mixing[:, 0]
    imag_part = mixing[:, 1]
    block_weight = jnp.concatenate(
        [
            jnp.concatenate([real_part, imag_part], axis=-1),
            jnp.concatenate([-imag_part, real_part], axis=-1),
        ],
        axis=1,
    )
    mixed = jnp.einsum("mlk,lkn->lmn", landed, block_weight, preferred_element_type=jnp.float32)
    return mixed.astype(jnp.bfloat16)


def solution(mesh):
    return jax.shard_map(
        on_device,
        mesh=mesh,
        in_specs=(
            P(("grp", "ord"), None, None),
            P("ord", None, None, None),
            P("ord", None, None, None),
        ),
        out_specs=P(("grp", "ord"), None, None),
        check_vma=False,
    )
```

profile of v0, /device:TPU:18, one launch (start us, length us, event | category | flops | bytes accessed | tf_op | source)
XLA Modules:
  0.0 919.4 jit_solution(554978800378174407)
XLA Ops:
  0.0 8.6 multiply_convert_fusion
  8.6 0.2 pad_maximum_fusion
  8.8 3.9 copy.20
  12.8 2.7 reshape.84
  15.5 25.9 %convert_bitcast_fusion = bf16[32,1024,256]{2,1,0:T(8,128)(2,1)} fusion(bf16[1024,1024,1]{0,1,2:T(8,128)(2,1)S(1)} %reshape.84, bf16[32,1024,256]{2,1,0:T(8,128)(2,1)} %param.5), kind=kOutput, calls=%fused_computation.12 | convolution fusion | flops 17188257792 | bytes 35651584 | tf_op jit(solution)/shard_map/tnc,nk->tkc/dot_general | solution.py:42
  41.4 24.5 %reshape.83 = bf16[32,512,512]{2,1,0:T(8,128)(2,1)} reshape(bf16[32,1024,256]{2,1,0:T(8,128)(2,1)} %convert_bitcast_fusion) | data formatting | bytes 33554432 | tf_op jit(solution)/shard_map/reshape | solution.py:45
  65.9 18.5 %copy.21 = bf16[32,512,512]{2,0,1:T(8,128)(2,1)} copy(bf16[32,512,512]{2,1,0:T(8,128)(2,1)} %reshape.83) | data formatting | bytes 33554432 | tf_op jit(solution)/shard_map/reshape | solution.py:45
  84.3 6.2 all-to-all-start
  90.5 13.7 %slice_bitcast_fusion = bf16[32,512,512]{2,1,0:T(8,128)(2,1)} fusion(bf16[1,64,512,512]{3,2,1,0:T(8,128)(2,1)} %param.6), kind=kLoop, calls=%fused_computation.13 | loop fusion | bytes 33554432 | tf_op jit(solution)/shard_map/slice | solution.py:48
  104.2 348.6 %all-to-all-done = bf16[32,512,512]{2,0,1:T(8,128)(2,1)} async-done(((bf16[32,512,512]{2,0,1:T(8,128)(2,1)}), bf16[32,512,512]{2,0,1:T(8,128)(2,1)}, u32[]{:S(2)}, u32[]{:S(2)}) %all-to-all-start) | async-done | bytes 16777248 | tf_op jit(solution)/shard_map/all_to_all | solution.py:46
  452.9 14.1 %copy.22 = bf16[16,32,32,512]{3,1,0,2:T(8,128)(2,1)} copy(bf16[16,32,32,512]{3,1,2,0:T(8,128)(2,1)} %bitcast.3) | data formatting | bytes 33554432 | tf_op jit(solution)/shard_map/all_to_all | solution.py:46
  466.9 6.1 broadcast_in_dim.2.clone
  473.1 27.6 %while.10 = (s32[]{:T(128)}, bf16[32,512,512]{2,0,1:T(8,128)(2,1)}, bf16[32,512,512]{2,1,0:T(8,128)(2,1)}, bf16[512,32,512]{2,0,1:T(8,128)(2,1)}, s32[]{:T(128)}, /*index=5*/s32[]{:T(128)}, s32[]{:T(128)}, s32[]{:T(128)}) while((s32[]{:T(128)}, bf16[32,512,512]{2,0,1:T(8,128)(2,1)}, bf16[32,512,512]{2,1,0:T(8,128)(2,1)}, ...), condition=%wide.region_1.2_spmd, body=%wide.region_0.1_spmd.sunk | while | flops 2147483648 | bytes 33554568 | solution.py:31
  473.1 9.4 %fusion.31 = bf16[32,128,512]{2,1,0:T(8,128)(2,1)S(1)} fusion(bf16[512,32,512]{2,0,1:T(8,128)(2,1)} %get-tuple-element.84, bf16[32,512,512]{2,1,0:T(8,128)(2,1)} %get-tuple-element.83, s32[]{:T(128)S(6)} %select_n.40), kind=kOutput, calls=%fused_computation.1.clone.1 | convolution fusion | flops 2147483648 | bytes 25165828 | tf_op jit(solution)/shard_map/while/body/mlt,tmk->mlk/dot_general | solution.py:28
  482.5 4.4 copy_dynamic-update-slice_fusion.2
  486.9 9.4 %fusion.31 = bf16[32,128,512]{2,1,0:T(8,128)(2,1)S(1)} fusion(bf16[512,32,512]{2,0,1:T(8,128)(2,1)} %get-tuple-element.84, bf16[32,512,512]{2,1,0:T(8,128)(2,1)} %get-tuple-element.83, s32[]{:T(128)S(6)} %select_n.40), kind=kOutput, calls=%fused_computation.1.clone.1 | convolution fusion | flops 2147483648 | bytes 25165828 | tf_op jit(solution)/shard_map/while/body/mlt,tmk->mlk/dot_general | solution.py:28
  496.3 4.4 copy_dynamic-update-slice_fusion.2
  500.6 17.6 %all-to-all-start.1 = ((bf16[32,512,512]{2,0,1:T(8,128)(2,1)}), bf16[32,512,512]{2,0,1:T(8,128)(2,1)}, u32[]{:S(2)}, u32[]{:S(2)}) async-start(bf16[32,512,512]{2,0,1:T(8,128)(2,1)} %get-tuple-element.27), calls=%async_computation.1 | async-start | bytes 33554432 | tf_op jit(solution)/shard_map/all_to_all | solution.py:49
  518.3 4.4 fusion.21
  522.7 5.9 slice_bitcast_fusion.1
  528.5 352.9 %all-to-all-done.1 = bf16[32,512,512]{2,0,1:T(8,128)(2,1)} async-done(((bf16[32,512,512]{2,0,1:T(8,128)(2,1)}), bf16[32,512,512]{2,0,1:T(8,128)(2,1)}, u32[]{:S(2)}, u32[]{:S(2)}) %all-to-all-start.1) | async-done | bytes 16777248 | tf_op jit(solution)/shard_map/all_to_all | solution.py:49
  881.4 0.0 copy-start
  881.4 14.4 %copy.24 = bf16[32,16,32,512]{3,0,1,2:T(8,128)(2,1)} copy(bf16[32,16,32,512]{3,0,2,1:T(8,128)(2,1)} %bitcast.5) | data formatting | bytes 33554432 | tf_op jit(solution)/shard_map/all_to_all | solution.py:49
  895.8 0.0 copy-done
  895.8 23.6 %fusion.11 = bf16[32,512,512]{2,1,0:T(8,128)(2,1)} fusion(bf16[512,32,512]{2,0,1:T(8,128)(2,1)} %bitcast.31, bf16[32,256,256]{2,1,0:T(8,128)(2,1)} %get-tuple-element.37, bf16[32,256,256]{2,1,0:T(8,128)(2,1)S(1)} %copy-done, bf16[32,256,256]{2,1,0:T(8,128)(2,1)} %get-tuple-element.36), kind=kOutput, calls=%fused_computation.14 | convolution fusion | flops 8665432064 | bytes 46137344 | tf_op jit(solution)/shard_map/mlk,lkn->lmn/dot_general | solution.py:59
Async XLA Ops:
  84.3 368.5 %all-to-all-start = ((bf16[32,512,512]{2,0,1:T(8,128)(2,1)}), bf16[32,512,512]{2,0,1:T(8,128)(2,1)}, u32[]{:S(2)}, u32[]{:S(2)}) async-start(bf16[32,512,512]{2,0,1:T(8,128)(2,1)} %copy.21), calls=%async_computation | async-start | bytes 33554432 | tf_op jit(solution)/shard_map/all_to_all | solution.py:46
  500.6 380.8 %all-to-all-start.1 = ((bf16[32,512,512]{2,0,1:T(8,128)(2,1)}), bf16[32,512,512]{2,0,1:T(8,128)(2,1)}, u32[]{:S(2)}, u32[]{:S(2)}) async-start(bf16[32,512,512]{2,0,1:T(8,128)(2,1)} %get-tuple-element.27), calls=%async_computation.1 | async-start | bytes 33554432 | tf_op jit(solution)/shard_map/all_to_all | solution.py:49
  881.4 14.4 %copy-start = (bf16[32,256,256]{2,1,0:T(8,128)(2,1)S(1)}, bf16[32,256,256]{2,1,0:T(8,128)(2,1)}, u32[]{:S(2)}) copy-start(bf16[32,256,256]{2,1,0:T(8,128)(2,1)} %fusion.21) | copy-start | bytes 12582916
where the time goes:
time: 921 us; the launch traced here: 919 us
  waiting for transfers between devices  701 us (76%)
  local copies, waits for them, and re-layouts  113 us (12%)
  matrix products  68.3 us (7%)
  starting transfers between devices  23.8 us (3%)
  other arithmetic  13.2 us (1%)
    all_to_all x1, waiting for transfers between devices, on_device(): lax.all_to_all(coeffs, 'ord', split_axis=1, concat_axis=0, tiled=True)  353 us
    all_to_all x1, waiting for transfers between devices, on_device(): lax.all_to_all(sending, 'ord', split_axis=1, concat_axis=0, tiled=True)  349 us
    reshape x2, local copies, waits for them, and re-layouts, on_device(): sending = spectra.reshape(lat_rows, orders, 2 * chans)  43 us
    dot_general x1, matrix products, on_device(): jnp.einsum('tnc,nk->tkc', grid, table, preferred_element_type=jnp.float32)  25.9 us
    dot_general x1, matrix products, on_device(): jnp.einsum('mlk,lkn->lmn', landed, block_weight, preferred_element_type=j...  23.6 us
    dot_general x2, matrix products, advance(): jnp.einsum('mlt,tmk->mlk', piece, arrived, preferred_element_type=jnp.flo...  18.8 us
  transfers between devices with their start and end apart: 2, of which 2 were waited for; matrix products, arithmetic and copies ran while one was open for 3% of the time, Pallas kernels for 0%

commit v1 on v0

--- a/solution.py
+++ b/solution.py
@@ -43,7 +43,10 @@
         jnp.bfloat16
     )
     sending = spectra.reshape(lat_rows, orders, 2 * chans)
-    arrived = lax.all_to_all(sending, "ord", split_axis=1, concat_axis=0, tiled=True)
+    arrived = jnp.concatenate(
+        lax.all_to_all(jnp.stack(jnp.split(sending, lax.axis_size("ord"), axis=1)), "ord", 0, 0),
+        axis=0,
+    )
     first = per_dev * block // DEG_TILE
     coeffs = legendre_tiles(panels[:per_dev], arrived, first)
     landed = lax.all_to_all(coeffs, "ord", split_axis=1, concat_axis=0, tiled=True)

time: 921 us -> 942 us (1.023)
  local copies, waits for them, and re-layouts: 113 us -> 134 us
    unnamed x2 -> x17, local copies, waits for them, and re-layouts: 0.01 us -> 34.6 us
    reshape x2 -> x1, local copies, waits for them, and re-layouts: 43 us -> 24.5 us  [on_device(): sending = spectra.reshape(lat_rows, orders, 2 * chans)]
where the time goes in v1:
time: 942 us; the launch traced here: 941 us
  waiting for transfers between devices  701 us (74%)
  local copies, waits for them, and re-layouts  134 us (14%)
  matrix products  68.3 us (7%)
  starting transfers between devices  23.8 us (3%)
  other arithmetic  13.2 us (1%)
    all_to_all x1, waiting for transfers between devices, on_device(): lax.all_to_all(coeffs, 'ord', split_axis=1, concat_axis=0, tiled=True)  353 us
    all_to_all x1, waiting for transfers between devices, on_device(): lax.all_to_all(jnp.stack(jnp.split(sending, lax.axis_size('ord'), axis=1)...  349 us
    unnamed x17, local copies, waits for them, and re-layouts  34.6 us
    dot_general x1, matrix products, on_device(): jnp.einsum('tnc,nk->tkc', grid, table, preferred_element_type=jnp.float32)  25.9 us
    reshape x1, local copies, waits for them, and re-layouts, on_device(): sending = spectra.reshape(lat_rows, orders, 2 * chans)  24.5 us
    dot_general x1, matrix products, on_device(): jnp.einsum('mlk,lkn->lmn', landed, block_weight, preferred_element_type=j...  23.6 us
  transfers between devices with their start and end apart: 2, of which 2 were waited for; matrix products, arithmetic and copies ran while one was open for 3% of the time, Pallas kernels for 0%

profile of v1, /device:TPU:18, one launch (start us, length us, event | category | flops | bytes accessed | tf_op | source)
XLA Modules:
  0.0 940.6 jit_solution(12287359795954431029)
XLA Ops:
  0.0 8.6 multiply_convert_fusion
  8.6 0.2 pad_maximum_fusion
  8.8 3.9 copy.18
  12.8 2.7 reshape.88
  15.5 25.9 %convert_bitcast_fusion = bf16[32,1024,256]{2,1,0:T(8,128)(2,1)} fusion(bf16[1024,1024,1]{0,1,2:T(8,128)(2,1)S(1)} %reshape.88, bf16[32,1024,256]{2,1,0:T(8,128)(2,1)} %param.5), kind=kOutput, calls=%fused_computation.12 | convolution fusion | flops 17188257792 | bytes 35651584 | tf_op jit(solution)/shard_map/tnc,nk->tkc/dot_general | solution.py:42
  41.4 24.5 %reshape.86 = bf16[32,512,512]{2,1,0:T(8,128)(2,1)} reshape(bf16[32,1024,256]{2,1,0:T(8,128)(2,1)} %convert_bitcast_fusion) | data formatting | bytes 33554432 | tf_op jit(solution)/shard_map/reshape | solution.py:45
  65.9 2.3 fusion.35
  68.2 2.3 fusion.34
  70.5 2.3 fusion.33
  72.8 2.3 fusion.32
  75.1 2.3 fusion.31
  77.4 2.3 fusion.30
  79.7 2.3 fusion.29
  82.0 2.3 fusion.28
  84.3 2.3 fusion.27
  86.6 2.3 fusion.26
  89.0 2.3 fusion.25
  91.3 2.3 fusion.24
  93.6 2.3 fusion.23
  95.9 2.3 fusion.22
  98.2 2.3 fusion.21
  100.5 2.3 fusion.20
  102.8 6.2 all-to-all-start
  109.0 13.7 %slice_bitcast_fusion = bf16[32,512,512]{2,1,0:T(8,128)(2,1)} fusion(bf16[1,64,512,512]{3,2,1,0:T(8,128)(2,1)} %param.6), kind=kLoop, calls=%fused_computation.13 | loop fusion | bytes 33554432 | tf_op jit(solution)/shard_map/slice | solution.py:51
  122.7 348.6 %all-to-all-done = bf16[16,32,32,512]{3,2,1,0:T(8,128)(2,1)} async-done(((bf16[16,32,32,512]{3,2,1,0:T(8,128)(2,1)}), bf16[16,32,32,512]{3,2,1,0:T(8,128)(2,1)}, u32[]{:S(2)}, u32[]{:S(2)}) %all-to-all-start) | async-done | bytes 16777248 | tf_op jit(solution)/shard_map/all_to_all | solution.py:47
  471.3 16.8 %copy.19 = bf16[16,32,32,512]{3,1,0,2:T(8,128)(2,1)} copy(bf16[16,32,32,512]{3,2,1,0:T(8,128)(2,1)} %all-to-all-done) | data formatting | bytes 33554432 | tf_op jit(solution)/shard_map/all_to_all | solution.py:47
  488.1 6.1 broadcast_in_dim.2.clone
  494.2 27.6 %while.10 = (s32[]{:T(128)}, bf16[32,512,512]{2,0,1:T(8,128)(2,1)}, bf16[32,512,512]{2,1,0:T(8,128)(2,1)}, bf16[512,32,512]{2,0,1:T(8,128)(2,1)}, s32[]{:T(128)}, /*index=5*/s32[]{:T(128)}, s32[]{:T(128)}, s32[]{:T(128)}) while((s32[]{:T(128)}, bf16[32,512,512]{2,0,1:T(8,128)(2,1)}, bf16[32,512,512]{2,1,0:T(8,128)(2,1)}, ...), condition=%wide.region_1.2_spmd, body=%wide.region_0.1_spmd.sunk | while | flops 2147483648 | bytes 33554568 | solution.py:31
  494.2 9.4 fusion.47
  503.6 4.4 copy_dynamic-update-slice_fusion.2
  508.0 9.4 fusion.47
  517.4 4.4 copy_dynamic-update-slice_fusion.2
  521.8 17.6 %all-to-all-start.1 = ((bf16[32,512,512]{2,0,1:T(8,128)(2,1)}), bf16[32,512,512]{2,0,1:T(8,128)(2,1)}, u32[]{:S(2)}, u32[]{:S(2)}) async-start(bf16[32,512,512]{2,0,1:T(8,128)(2,1)} %get-tuple-element.27), calls=%async_computation.1 | async-start | bytes 33554432 | tf_op jit(solution)/shard_map/all_to_all | solution.py:52
  539.4 4.4 fusion.37
  543.8 5.9 slice_bitcast_fusion.1
  549.7 352.9 %all-to-all-done.1 = bf16[32,512,512]{2,0,1:T(8,128)(2,1)} async-done(((bf16[32,512,512]{2,0,1:T(8,128)(2,1)}), bf16[32,512,512]{2,0,1:T(8,128)(2,1)}, u32[]{:S(2)}, u32[]{:S(2)}) %all-to-all-start.1) | async-done | bytes 16777248 | tf_op jit(solution)/shard_map/all_to_all | solution.py:52
  902.5 0.0 copy-start
  902.6 14.4 %copy.21 = bf16[32,16,32,512]{3,0,1,2:T(8,128)(2,1)} copy(bf16[32,16,32,512]{3,0,2,1:T(8,128)(2,1)} %bitcast.19) | data formatting | bytes 33554432 | tf_op jit(solution)/shard_map/all_to_all | solution.py:52
  916.9 0.0 copy-done
  916.9 23.6 %fusion.11 = bf16[32,512,512]{2,1,0:T(8,128)(2,1)} fusion(bf16[512,32,512]{2,0,1:T(8,128)(2,1)} %bitcast.92, bf16[32,256,256]{2,1,0:T(8,128)(2,1)} %get-tuple-element.37, bf16[32,256,256]{2,1,0:T(8,128)(2,1)S(1)} %copy-done, bf16[32,256,256]{2,1,0:T(8,128)(2,1)} %get-tuple-element.36), kind=kOutput, calls=%fused_computation.14 | convolution fusion | flops 8665432064 | bytes 46137344 | tf_op jit(solution)/shard_map/mlk,lkn->lmn/dot_general | solution.py:62
Async XLA Ops:
  102.8 368.5 %all-to-all-start = ((bf16[16,32,32,512]{3,2,1,0:T(8,128)(2,1)}), bf16[16,32,32,512]{3,2,1,0:T(8,128)(2,1)}, u32[]{:S(2)}, u32[]{:S(2)}) async-start(bf16[16,32,32,512]{3,2,1,0:T(8,128)(2,1)} %fusion.20), calls=%async_computation | async-start | bytes 33554432 | tf_op jit(solution)/shard_map/all_to_all | solution.py:47
  521.8 380.8 %all-to-all-start.1 = ((bf16[32,512,512]{2,0,1:T(8,128)(2,1)}), bf16[32,512,512]{2,0,1:T(8,128)(2,1)}, u32[]{:S(2)}, u32[]{:S(2)}) async-start(bf16[32,512,512]{2,0,1:T(8,128)(2,1)} %get-tuple-element.27), calls=%async_computation.1 | async-start | bytes 33554432 | tf_op jit(solution)/shard_map/all_to_all | solution.py:52
  902.5 14.4 %copy-start = (bf16[32,256,256]{2,1,0:T(8,128)(2,1)S(1)}, bf16[32,256,256]{2,1,0:T(8,128)(2,1)}, u32[]{:S(2)}) copy-start(bf16[32,256,256]{2,1,0:T(8,128)(2,1)} %fusion.37) | copy-start | bytes 12582916
